TPU v7x, 256 devices: a whole 4x4x8 slice. The times are simulated.
256 devices in a mesh: dp: 16 (over y, z_hi), mp: 16 (over x, z_lo, core).
Axes of the slice: x: 4, y: 4, z: 8 (z_hi: 4, z_lo: 2; z = z_hi * 2 + z_lo), core: 2. Of those that a mesh axis runs over, the one named last changes fastest.
Arguments:
- tokens: bfloat16 [4096, 4096], P('dp', 'mp'), may hold values from -6 to 6
- norm_gain: float32 [4096], P('mp'), may hold values from 0.75 to 7.5
- w_gate: bfloat16 [4096, 6144], P('dp', 'mp'), may hold values from -0.09375 to 0.09375
- w_up: bfloat16 [4096, 6144], P('dp', 'mp'), may hold values from -0.09375 to 0.09375
- cotangent: bfloat16 [4096, 6144], P('dp', 'mp'), may hold values from -0.09375 to 0.09375
- decay_mask: int32 [2, 4096], replicated, may hold values 0 or 1
- radius: float32 [1], replicated, may hold values from 12.8 to 38.4
Outputs:
- grad_gain: float32 [4096], P('mp')
- grad_gate: float32 [4096, 6144], P('dp', 'mp')
- grad_up: float32 [4096, 6144], P('dp', 'mp')
Inputs may be any that keep to these rules, and one draw needn't show every extreme that they name: `decay_mask`: 1 marks a row that is perturbed.
All inputs are finite; a program needn't handle non-finite values.
Results may differ from a plain program's by a relative error of at most 0.024.
Values may be sent and summed in bfloat16 or wider, within the bound.
No kernel may reach another device: no remote copies, remote signals or barrier semaphores. Data moves between devices by JAX's collectives and lax.ppermute only.
A program may use at most 64 MiB of HBM per device.

v0:
```python
import jax
import jax.numpy as jnp
from jax import lax
from jax.sharding import PartitionSpec as P


def activation(value):
    return jax.nn.gelu(value, approximate=True)


def fetch_weights(part_gate, part_up):
    return (
        lax.all_gather(part_gate, "dp", axis=0, tiled=True),
        lax.all_gather(part_up, "dp", axis=0, tiled=True),
    )


def one_pass(scaled_rows, gain_part, full_gate, full_up, cotangent):
    hidden_width = full_gate.shape[1]
    normed_part = (scaled_rows * gain_part[None, :]).astype(jnp.bfloat16)
    normed = lax.all_gather(normed_part, "mp", axis=1, tiled=True)
    pre_gate = jnp.dot(normed, full_gate, preferred_element_type=jnp.float32)
    pre_up = jnp.dot(normed, full_up, preferred_element_type=jnp.float32)
    activated, back_fn = jax.vjp(activation, pre_gate)
    upstream = cotangent.astype(jnp.float32)
    d_up = (upstream * activated).astype(jnp.bfloat16)
    d_gate = back_fn(upstream * pre_up)[0].astype(jnp.bfloat16)
    feature_term = lax.dot_general(
        d_gate, full_gate, (((1,), (1,)), ((), ())), preferred_element_type=jnp.float32
    )
    feature_term = feature_term + lax.dot_general(
        d_up, full_up, (((1,), (1,)), ((), ())), preferred_element_type=jnp.float32
    )
    d_norm = lax.psum_scatter(
        feature_term.astype(jnp.bfloat16), "mp", scatter_dimension=1, tiled=True
    ).astype(jnp.float32)
    d_gain = lax.psum(jnp.sum(d_norm * scaled_rows, axis=0), "dp")
    stacked = jnp.concatenate([d_gate, d_up], axis=1)
    both = lax.psum_scatter(
        lax.dot_general(
            normed, stacked, (((0,), (0,)), ((), ())), preferred_element_type=jnp.float32
        ).astype(jnp.bfloat16),
        "dp",
        scatter_dimension=0,
        tiled=True,
    ).astype(jnp.float32)
    return (d_gain, both[:, :hidden_width], both[:, hidden_width:])


def body(tokens, norm_gain, w_gate, w_up, cotangent, decay_mask, radius):
    values = tokens.astype(jnp.float32)
    width = values.shape[1] * lax.axis_size("mp")
    row_total = lax.psum(jnp.sum(values * values, axis=1), "mp")
    scaled_rows = values * lax.rsqrt(row_total / width + 1e-06)[:, None]
    groups = decay_mask.astype(jnp.float32)
    local_rows = w_gate.shape[0]
    first_row = lax.axis_index("dp") * local_rows
    local_groups = lax.dynamic_slice_in_dim(groups, first_row, local_rows, 1)
    gate_mask = local_groups[0][:, None]
    up_mask = local_groups[1][:, None]
    full_gate, full_up = fetch_weights(w_gate, w_up)
    asc_gain, asc_gate_f, asc_up_f = one_pass(scaled_rows, norm_gain, full_gate, full_up, cotangent)
    gate_low = asc_gate_f.astype(jnp.bfloat16)
    up_low = asc_up_f.astype(jnp.bfloat16)
    gate_wide = gate_low.astype(jnp.float32)
    up_wide = up_low.astype(jnp.float32)
    matrix_part = jnp.sum(gate_mask * gate_wide * gate_wide) + jnp.sum(up_mask * up_wide * up_wide)
    total = lax.psum(matrix_part, ("dp", "mp"))
    factor = radius[0] / (jnp.sqrt(total) + 1e-12)
    new_gate = (w_gate.astype(jnp.float32) + factor * gate_mask * gate_wide).astype(jnp.bfloat16)
    new_up = (w_up.astype(jnp.float32) + factor * up_mask * up_wide).astype(jnp.bfloat16)
    next_gate, next_up = fetch_weights(new_gate, new_up)
    return one_pass(scaled_rows, norm_gain, next_gate, next_up, cotangent)


def solution(mesh):
    placed = (P("dp", "mp"), P("mp"), P("dp", "mp"), P("dp", "mp"), P("dp", "mp"), P(), P())
    return jax.shard_map(
        body,
        mesh=mesh,
        in_specs=placed,
        out_specs=(P("mp"), P("dp", "mp"), P("dp", "mp")),
        check_vma=False,
    )
```

profile of v0, /device:TPU:1, one launch (start us, length us, event | category | flops | bytes accessed | tf_op | source)
XLA Modules:
  0.0 741.6 jit_solution(15227484376641133650)
XLA Ops:
  8.2 29.7 %psum.21 = f32[256]{0:T(256)S(1)} all-reduce(f32[256]{0:T(256)S(1)} %fusion.33), channel_id=1, replica_groups=mesh['dp'=16,'mp'=16] {'mp'}, use_global_device_ids=true, to_apply=%region_1.0 | all-reduce | flops 256 | bytes 2048 | tf_op jit(solution)/shard_map/psum | solution.py:53
  38.0 1.7 fusion.31
  41.2 40.3 %all-gather.6.cloned.1.call-done = bf16[256,4096]{1,0:T(8,128)(2,1)} async-done(((bf16[256,256]{1,0:T(8,128)(2,1)}), bf16[256,4096]{1,0:T(8,128)(2,1)}) %all-gather.6.cloned.1.call-update) | async-done | bytes 2097168 | tf_op jit(solution)/shard_map/all_gather | solution.py:21
  81.5 69.6 %all-gather.10.cloned.1.call-done = bf16[4096,384]{1,0:T(8,128)(2,1)} async-done(((bf16[256,384]{1,0:T(8,128)(2,1)}), bf16[4096,384]{1,0:T(8,128)(2,1)}) %all-gather.10.cloned.1.call-update) | async-done | bytes 3145744 | tf_op jit(solution)/shard_map/all_gather | solution.py:13
  151.1 3.9 fusion.21
  155.0 64.3 %all-gather.8.cloned.1.call-done = bf16[4096,384]{1,0:T(8,128)(2,1)} async-done(((bf16[256,384]{1,0:T(8,128)(2,1)}), bf16[4096,384]{1,0:T(8,128)(2,1)}) %all-gather.8.cloned.1.call-update) | async-done | bytes 3145744 | tf_op jit(solution)/shard_map/all_gather | solution.py:14
  219.4 3.3 fusion.11
  222.7 4.5 convolution_convert_fusion.1
  228.1 107.1 %reduce-scatter.4.cloned.1.call-done = bf16[256,768]{1,0:T(8,128)(2,1)} async-done(((bf16[4096,768]{1,0:T(8,128)(2,1)}), bf16[256,768]{1,0:T(8,128)(2,1)}) %reduce-scatter.4.cloned.1.call-update) | async-done | bytes 393232 | tf_op jit(solution)/shard_map/reduce_scatter | solution.py:39
  335.2 1.9 fusion.20
  339.0 75.6 %psum.22 = f32[]{:T(128)} all-reduce(f32[]{:T(128)S(6)} %add.55), channel_id=1, replica_groups=mesh['dp'=16,'mp'=16] {'dp','mp'}, use_global_device_ids=true, to_apply=%region_5.0 | all-reduce | flops 1 | bytes 8 | tf_op jit(solution)/shard_map/psum | solution.py:68
  415.4 2.0 fusion.4
  418.0 62.4 %all-gather.14.cloned.1.call-done = bf16[4096,384]{1,0:T(8,128)(2,1)} async-done(((bf16[256,384]{1,0:T(8,128)(2,1)}), bf16[4096,384]{1,0:T(8,128)(2,1)}) %all-gather.14.cloned.1.call-update) | async-done | bytes 3145744 | tf_op jit(solution)/shard_map/all_gather | solution.py:13
  480.5 3.3 fusion.22
  483.7 65.4 %all-gather.12.cloned.1.call-done = bf16[4096,384]{1,0:T(8,128)(2,1)} async-done(((bf16[256,384]{1,0:T(8,128)(2,1)}), bf16[4096,384]{1,0:T(8,128)(2,1)}) %all-gather.12.cloned.1.call-update) | async-done | bytes 3145744 | tf_op jit(solution)/shard_map/all_gather | solution.py:14
  549.1 3.5 fusion.18
  552.6 1.3 fusion.38
  554.5 2.7 fusion
  557.3 4.5 convolution_convert_fusion
  561.8 57.3 %reduce-scatter.6.cloned.1.call-done = bf16[256,256]{1,0:T(8,128)(2,1)} async-done(((bf16[256,4096]{1,0:T(8,128)(2,1)}), bf16[256,256]{1,0:T(8,128)(2,1)}) %reduce-scatter.6.cloned.1.call-update) | async-done | bytes 131088 | tf_op jit(solution)/shard_map/reduce_scatter | solution.py:34
  619.2 1.0 fusion.32
  620.2 39.4 %psum.23 = f32[256]{0:T(256)} all-reduce(f32[256]{0:T(256)S(1)} %fusion.32), channel_id=1, replica_groups=mesh['dp'=16,'mp'=16] {'dp'}, use_global_device_ids=true, to_apply=%region_8.0 | all-reduce | flops 256 | bytes 2048 | tf_op jit(solution)/shard_map/psum | solution.py:37
  659.6 73.1 %reduce-scatter.8.cloned.1.call-done = bf16[256,768]{1,0:T(8,128)(2,1)} async-done(((bf16[4096,768]{1,0:T(8,128)(2,1)}), bf16[256,768]{1,0:T(8,128)(2,1)}) %reduce-scatter.8.cloned.1.call-update) | async-done | bytes 393232 | tf_op jit(solution)/shard_map/reduce_scatter | solution.py:39
  732.8 1.9 fusion.36
  (35 shorter events, 4.7 us)
Async XLA Ops:
  7.2 74.4 %all-gather.6.cloned.1.call-start = ((), (), s32[]{:S(2)}) async-start(), calls=%async_computation.3 | async-start | bytes 2228224 | tf_op jit(solution)/shard_map/all_gather | solution.py:21
  39.7 111.4 %all-gather.10.cloned.1.call-start = ((), (), s32[]{:S(2)}) async-start(), calls=%async_computation.5 | async-start | bytes 3342336 | tf_op jit(solution)/shard_map/all_gather | solution.py:13
  40.4 178.9 %all-gather.8.cloned.1.call-start = ((), (), s32[]{:S(2)}) async-start(), calls=%async_computation.4 | async-start | bytes 3342336 | tf_op jit(solution)/shard_map/all_gather | solution.py:14
  41.2 178.2 %copy-start.6 = (bf16[256,384]{1,0:T(8,128)(2,1)S(1)}, bf16[256,384]{1,0:T(8,128)(2,1)}, u32[]{:S(2)}) copy-start(bf16[256,384]{1,0:T(8,128)(2,1)} %param.11) | copy-start | bytes 589828
  41.2 294.1 %reduce-scatter.4.cloned.1.call-start = ((), (), s32[]{:S(2)}) async-start(), calls=%async_computation.6 | async-start | bytes 6684672 | tf_op jit(solution)/shard_map/reduce_scatter | solution.py:39
  81.5 137.8 %copy-start = (bf16[256,4096]{1,0:T(8,128)(2,1)S(1)}, bf16[256,4096]{1,0:T(8,128)(2,1)}, u32[]{:S(2)}) copy-start(bf16[256,4096]{1,0:T(8,128)(2,1)} %all-gather.6.cloned.1.call-done) | copy-start | bytes 6291460
  227.2 188.2 %copy-start.4 = (bf16[256,384]{1,0:T(8,128)(2,1)S(1)}, bf16[256,384]{1,0:T(8,128)(2,1)}, u32[]{:S(2)}) copy-start(bf16[256,384]{1,0:T(8,128)(2,1)} %param.9) | copy-start | bytes 589828
  227.2 188.2 %copy-start.5 = (bf16[256,384]{1,0:T(8,128)(2,1)S(1)}, bf16[256,384]{1,0:T(8,128)(2,1)}, u32[]{:S(2)}) copy-start(bf16[256,384]{1,0:T(8,128)(2,1)} %param.10) | copy-start | bytes 589828
  227.3 253.2 %all-gather.14.cloned.1.call-start = ((), (), s32[]{:S(2)}) async-start(), calls=%async_computation.8 | async-start | bytes 3342336 | tf_op jit(solution)/shard_map/all_gather | solution.py:13
  417.4 131.7 %all-gather.12.cloned.1.call-start = ((), (), s32[]{:S(2)}) async-start(), calls=%async_computation.7 | async-start | bytes 3342336 | tf_op jit(solution)/shard_map/all_gather | solution.py:14
  418.0 201.2 %reduce-scatter.6.cloned.1.call-start = ((), (), s32[]{:S(2)}) async-start(), calls=%async_computation.9 | async-start | bytes 2228224 | tf_op jit(solution)/shard_map/reduce_scatter | solution.py:34
  549.1 3.5 copy-start.1
  552.6 1.9 copy-start.2
  557.2 175.5 %reduce-scatter.8.cloned.1.call-start = ((), (), s32[]{:S(2)}) async-start(), calls=%async_computation.10 | async-start | bytes 6684672 | tf_op jit(solution)/shard_map/reduce_scatter | solution.py:39
  561.8 57.4 %copy-start.3 = (bf16[256,256]{1,0:T(8,128)(2,1)S(1)}, bf16[256,256]{1,0:T(8,128)(2,1)}, u32[]{:S(2)}) copy-start(bf16[256,256]{1,0:T(8,128)(2,1)} %param.7) | copy-start | bytes 393220
Sparse Core Ops, SparseCore 0:
  39.8 41.6 all-gather.5
  84.0 67.0 all-gather.9
  153.6 65.7 all-gather.7
  227.4 107.7 reduce-scatter.3
  417.5 62.9 all-gather.13
  483.4 65.7 all-gather.11
  557.3 61.7 reduce-scatter.5
  622.9 109.8 reduce-scatter.7
where the time goes:
time: 742 us
  waiting for transfers between devices  542 us (73%)
  blocking collectives  145 us (20%)
  matrix products  27.1 us (4%)
  between operations  16.9 us (2%)
  other arithmetic  8.34 us (1%)
    reduce_scatter x2, waiting for transfers between devices, one_pass(): lax.psum_scatter(lax.dot_general(normed, stacked, (((0,), (0,)), ((), ())...  180 us
    all_gather x2, waiting for transfers between devices, fetch_weights(): lax.all_gather(part_gate, 'dp', axis=0, tiled=True)  132 us
    all_gather x2, waiting for transfers between devices, fetch_weights(): lax.all_gather(part_up, 'dp', axis=0, tiled=True)  130 us
    psum x1, blocking collectives, body(): total = lax.psum(matrix_part, ('dp', 'mp'))  75.6 us
    reduce_scatter x1, waiting for transfers between devices, one_pass(): lax.psum_scatter(feature_term.astype(jnp.bfloat16), 'mp', scatter_dimensi...  57.3 us
    all_gather x1, waiting for transfers between devices, one_pass(): normed = lax.all_gather(normed_part, 'mp', axis=1, tiled=True)  40.3 us
    psum x1, blocking collectives, one_pass(): d_gain = lax.psum(jnp.sum(d_norm * scaled_rows, axis=0), 'dp')  39.4 us
    psum x1, blocking collectives, body(): row_total = lax.psum(jnp.sum(values * values, axis=1), 'mp')  29.7 us
  transfers between devices with their start and end apart: 8, of which 8 were waited for; matrix products, arithmetic and copies ran while one was open for 2% of the time, Pallas kernels for 0%

commit v1 on v0

--- a/solution.py
+++ b/solution.py
@@ -10,7 +10,9 @@
 
 def fetch_weights(part_gate, part_up):
     return (
-        lax.all_gather(part_gate, "dp", axis=0, tiled=True),
+        jnp.concatenate(
+            lax.all_to_all(jnp.stack([part_gate] * lax.axis_size("dp")), "dp", 0, 0), axis=0
+        ),
         lax.all_gather(part_up, "dp", axis=0, tiled=True),
     )
 

time: 742 us -> 687 us (0.926)
  waiting for transfers between devices: 542 us -> 463 us
  starting transfers between devices: 0.32 us -> 14.7 us
    all_gather x2 -> x0, waiting for transfers between devices: 132 us -> none  [fetch_weights(): lax.all_gather(part_gate, 'dp', axis=0, tiled=True)]
    all_to_all x0 -> x2, waiting for transfers between devices: none -> 96.7 us  [fetch_weights(): lax.all_to_all(jnp.stack([part_gate] * lax.axis_size('dp')), 'dp', 0, 0)]
    all_gather x2, waiting for transfers between devices: 130 us -> 74.8 us  [fetch_weights(): lax.all_gather(part_up, 'dp', axis=0, tiled=True)]
    all_to_all x0 -> x2, starting transfers between devices: none -> 14.3 us  [fetch_weights(): lax.all_to_all(jnp.stack([part_gate] * lax.axis_size('dp')), 'dp', 0, 0)]
    all_gather x1, waiting for transfers between devices: 40.3 us -> 52.5 us  [one_pass(): normed = lax.all_gather(normed_part, 'mp', axis=1, tiled=True)]
where the time goes in v1:
time: 687 us; the launch traced here: 686 us
  waiting for transfers between devices  463 us (67%)
  blocking collectives  145 us (21%)
  matrix products  29.2 us (4%)
  between operations  16.9 us (2%)
  starting transfers between devices  14.7 us (2%)
  local copies, waits for them, and re-layouts  8.78 us (1%)
  other arithmetic  8.19 us (1%)
    reduce_scatter x2, waiting for transfers between devices, one_pass(): lax.psum_scatter(lax.dot_general(normed, stacked, (((0,), (0,)), ((), ())...  180 us
    all_to_all x2, waiting for transfers between devices, fetch_weights(): lax.all_to_all(jnp.stack([part_gate] * lax.axis_size('dp')), 'dp', 0, 0)  96.7 us
    psum x1, blocking collectives, body(): total = lax.psum(matrix_part, ('dp', 'mp'))  75.6 us
    all_gather x2, waiting for transfers between devices, fetch_weights(): lax.all_gather(part_up, 'dp', axis=0, tiled=True)  74.8 us
    reduce_scatter x1, waiting for transfers between devices, one_pass(): lax.psum_scatter(feature_term.astype(jnp.bfloat16), 'mp', scatter_dimensi...  58.2 us
    all_gather x1, waiting for transfers between devices, one_pass(): normed = lax.all_gather(normed_part, 'mp', axis=1, tiled=True)  52.5 us
    psum x1, blocking collectives, one_pass(): d_gain = lax.psum(jnp.sum(d_norm * scaled_rows, axis=0), 'dp')  39.7 us
    psum x1, blocking collectives, body(): row_total = lax.psum(jnp.sum(values * values, axis=1), 'mp')  29.7 us
  transfers between devices with their start and end apart: 8, of which 8 were waited for; matrix products, arithmetic and copies ran while one was open for 2% of the time, Pallas kernels for 0%

profile of v1, /device:TPU:1, one launch (start us, length us, event | category | flops | bytes accessed | tf_op | source)
XLA Modules:
  0.0 686.1 jit_solution(17362352662696367271)
XLA Ops:
  8.2 29.7 %psum.21 = f32[256]{0:T(256)S(1)} all-reduce(f32[256]{0:T(256)S(1)} %fusion.33), channel_id=1, replica_groups=mesh['dp'=16,'mp'=16] {'mp'}, use_global_device_ids=true, to_apply=%region_1.0 | all-reduce | flops 256 | bytes 2048 | tf_op jit(solution)/shard_map/psum | solution.py:55
  39.7 3.0 stack.4
  42.7 9.3 %all-to-all-start = ((bf16[16,256,384]{2,1,0:T(8,128)(2,1)}), bf16[16,256,384]{2,1,0:T(8,128)(2,1)S(1)}, u32[]{:S(2)}, u32[]{:S(2)}) async-start(bf16[16,256,384]{2,1,0:T(8,128)(2,1)} %stack.4), calls=%async_computation | async-start | bytes 6291456 | tf_op jit(solution)/shard_map/all_to_all | solution.py:14
  52.8 52.5 %all-gather.4.cloned.1.call-done = bf16[256,4096]{1,0:T(8,128)(2,1)} async-done(((bf16[256,256]{1,0:T(8,128)(2,1)}), bf16[256,4096]{1,0:T(8,128)(2,1)}) %all-gather.4.cloned.1.call-update) | async-done | bytes 2097168 | tf_op jit(solution)/shard_map/all_gather | solution.py:23
  105.3 28.8 %all-to-all-done = bf16[16,256,384]{2,1,0:T(8,128)(2,1)S(1)} async-done(((bf16[16,256,384]{2,1,0:T(8,128)(2,1)}), bf16[16,256,384]{2,1,0:T(8,128)(2,1)S(1)}, u32[]{:S(2)}, u32[]{:S(2)}) %all-to-all-start) | async-done | bytes 3145760 | tf_op jit(solution)/shard_map/all_to_all | solution.py:14
  135.8 4.0 fusion.21
  139.8 42.0 %all-gather.6.cloned.1.call-done = bf16[4096,384]{1,0:T(8,128)(2,1)} async-done(((bf16[256,384]{1,0:T(8,128)(2,1)}), bf16[4096,384]{1,0:T(8,128)(2,1)}) %all-gather.6.cloned.1.call-update) | async-done | bytes 3145744 | tf_op jit(solution)/shard_map/all_gather | solution.py:16
  181.8 3.3 fusion.11
  185.2 4.5 convolution_convert_fusion.1
  190.5 106.9 %reduce-scatter.4.cloned.1.call-done = bf16[256,768]{1,0:T(8,128)(2,1)} async-done(((bf16[4096,768]{1,0:T(8,128)(2,1)}), bf16[256,768]{1,0:T(8,128)(2,1)}) %reduce-scatter.4.cloned.1.call-update) | async-done | bytes 393232 | tf_op jit(solution)/shard_map/reduce_scatter | solution.py:41
  301.2 75.6 %psum.22 = f32[]{:T(128)} all-reduce(f32[]{:T(128)S(6)} %add.55), channel_id=1, replica_groups=mesh['dp'=16,'mp'=16] {'dp','mp'}, use_global_device_ids=true, to_apply=%region_5.0 | all-reduce | flops 1 | bytes 8 | tf_op jit(solution)/shard_map/psum | solution.py:70
  379.4 2.1 stack.5
  381.5 5.0 all-to-all-start.1
  387.2 67.9 %all-to-all-done.1 = bf16[16,256,384]{2,1,0:T(8,128)(2,1)} async-done(((bf16[16,256,384]{2,1,0:T(8,128)(2,1)}), bf16[16,256,384]{2,1,0:T(8,128)(2,1)}, u32[]{:S(2)}, u32[]{:S(2)}) %all-to-all-start.1) | async-done | bytes 3145760 | tf_op jit(solution)/shard_map/all_to_all | solution.py:14
  455.2 3.4 fusion.22
  458.6 32.7 %all-gather.8.cloned.1.call-done = bf16[4096,384]{1,0:T(8,128)(2,1)} async-done(((bf16[256,384]{1,0:T(8,128)(2,1)}), bf16[4096,384]{1,0:T(8,128)(2,1)}) %all-gather.8.cloned.1.call-update) | async-done | bytes 3145744 | tf_op jit(solution)/shard_map/all_gather | solution.py:16
  491.3 3.3 fusion.18
  494.7 3.3 fusion.38
  498.0 2.7 fusion
  500.8 4.5 convolution_convert_fusion
  505.3 58.2 %reduce-scatter.6.cloned.1.call-done = bf16[256,256]{1,0:T(8,128)(2,1)} async-done(((bf16[256,4096]{1,0:T(8,128)(2,1)}), bf16[256,256]{1,0:T(8,128)(2,1)}) %reduce-scatter.6.cloned.1.call-update) | async-done | bytes 131088 | tf_op jit(solution)/shard_map/reduce_scatter | solution.py:36
  564.6 39.7 %psum.23 = f32[256]{0:T(256)} all-reduce(f32[256]{0:T(256)S(1)} %fusion.32), channel_id=1, replica_groups=mesh['dp'=16,'mp'=16] {'dp'}, use_global_device_ids=true, to_apply=%region_8.0 | all-reduce | flops 256 | bytes 2048 | tf_op jit(solution)/shard_map/psum | solution.py:39
  604.3 73.1 %reduce-scatter.8.cloned.1.call-done = bf16[256,768]{1,0:T(8,128)(2,1)} async-done(((bf16[4096,768]{1,0:T(8,128)(2,1)}), bf16[256,768]{1,0:T(8,128)(2,1)}) %reduce-scatter.8.cloned.1.call-update) | async-done | bytes 393232 | tf_op jit(solution)/shard_map/reduce_scatter | solution.py:41
  677.4 1.9 fusion.36
  (35 shorter events, 11.6 us)
Async XLA Ops:
  7.2 98.1 %all-gather.4.cloned.1.call-start = ((), (), s32[]{:S(2)}) async-start(), calls=%async_computation.5 | async-start | bytes 2228224 | tf_op jit(solution)/shard_map/all_gather | solution.py:23
  42.7 93.1 %copy-start.6 = (bf16[256,384]{1,0:T(8,128)(2,1)S(1)}, bf16[256,384]{1,0:T(8,128)(2,1)}, u32[]{:S(2)}) copy-start(bf16[256,384]{1,0:T(8,128)(2,1)} %param.11) | copy-start | bytes 589828
  42.7 91.4 %all-to-all-start = ((bf16[16,256,384]{2,1,0:T(8,128)(2,1)}), bf16[16,256,384]{2,1,0:T(8,128)(2,1)S(1)}, u32[]{:S(2)}, u32[]{:S(2)}) async-start(bf16[16,256,384]{2,1,0:T(8,128)(2,1)} %stack.4), calls=%async_computation | async-start | bytes 6291456 | tf_op jit(solution)/shard_map/all_to_all | solution.py:14
  52.0 129.8 %all-gather.6.cloned.1.call-start = ((), (), s32[]{:S(2)}) async-start(), calls=%async_computation.6 | async-start | bytes 3342336 | tf_op jit(solution)/shard_map/all_gather | solution.py:16
  52.8 244.6 %reduce-scatter.4.cloned.1.call-start = ((), (), s32[]{:S(2)}) async-start(), calls=%async_computation.7 | async-start | bytes 6684672 | tf_op jit(solution)/shard_map/reduce_scatter | solution.py:41
  134.1 1.7 copy-start.1
  135.8 46.1 %copy-start = (bf16[256,4096]{1,0:T(8,128)(2,1)S(1)}, bf16[256,4096]{1,0:T(8,128)(2,1)}, u32[]{:S(2)}) copy-start(bf16[256,4096]{1,0:T(8,128)(2,1)} %all-gather.4.cloned.1.call-done) | copy-start | bytes 6291460
  189.7 187.8 %copy-start.4 = (bf16[256,384]{1,0:T(8,128)(2,1)S(1)}, bf16[256,384]{1,0:T(8,128)(2,1)}, u32[]{:S(2)}) copy-start(bf16[256,384]{1,0:T(8,128)(2,1)} %param.9) | copy-start | bytes 589828
  189.7 187.8 %copy-start.5 = (bf16[256,384]{1,0:T(8,128)(2,1)S(1)}, bf16[256,384]{1,0:T(8,128)(2,1)}, u32[]{:S(2)}) copy-start(bf16[256,384]{1,0:T(8,128)(2,1)} %param.10) | copy-start | bytes 589828
  381.5 73.7 %all-to-all-start.1 = ((bf16[16,256,384]{2,1,0:T(8,128)(2,1)}), bf16[16,256,384]{2,1,0:T(8,128)(2,1)}, u32[]{:S(2)}, u32[]{:S(2)}) async-start(bf16[16,256,384]{2,1,0:T(8,128)(2,1)} %stack.5), calls=%async_computation.2 | async-start | bytes 6291456 | tf_op jit(solution)/shard_map/all_to_all | solution.py:14
  386.4 104.9 %all-gather.8.cloned.1.call-start = ((), (), s32[]{:S(2)}) async-start(), calls=%async_computation.8 | async-start | bytes 3342336 | tf_op jit(solution)/shard_map/all_gather | solution.py:16
  387.0 176.5 %reduce-scatter.6.cloned.1.call-start = ((), (), s32[]{:S(2)}) async-start(), calls=%async_computation.9 | async-start | bytes 2228224 | tf_op jit(solution)/shard_map/reduce_scatter | solution.py:36
  494.7 3.3 copy-start.2
  500.7 176.6 %reduce-scatter.8.cloned.1.call-start = ((), (), s32[]{:S(2)}) async-start(), calls=%async_computation.10 | async-start | bytes 6684672 | tf_op jit(solution)/shard_map/reduce_scatter | solution.py:41
  505.3 58.2 %copy-start.3 = (bf16[256,256]{1,0:T(8,128)(2,1)S(1)}, bf16[256,256]{1,0:T(8,128)(2,1)}, u32[]{:S(2)}) copy-start(bf16[256,256]{1,0:T(8,128)(2,1)} %param.7) | copy-start | bytes 393220
Sparse Core Ops, SparseCore 0:
  39.8 65.4 all-gather.3
  107.8 74.0 all-gather.5
  189.8 107.4 reduce-scatter.3
  390.0 101.2 all-gather.7
  500.8 62.6 reduce-scatter.5
  567.1 110.1 reduce-scatter.7
